TPU v7x, 32 devices: a whole 2x2x4 slice. The times are simulated.
32 devices in a mesh: ia: 4 (over z), ja: 8 (over y, x, core).
Axes of the slice: x: 2, y: 2, z: 4, core: 2. Of those that a mesh axis runs over, the one named last changes fastest.
Arguments:
- pno_basis: bfloat16 [4, 16, 512, 128], P('ia', 'ja'), may hold values from -0.4375 to 0.4375
- domain_map: int32 [4, 16, 512], replicated, may hold values from 0 to 1023, as said below
- amplitudes: float32 [4, 16, 128, 128], P('ia', 'ja'), may hold values from -6 to 6
- exchange_ints: float32 [4, 16, 128, 128], P('ia', 'ja'), may hold values from -6 to 6
- pno_energy: float32 [4, 16, 128], P('ia', 'ja'), may hold values from 0.5 to 3
- row_energy: float32 [4], P('ia'), may hold values from -1.5 to -0.3
- column_energy: float32 [16], P('ja'), may hold values from -1.5 to -0.3
- coupling_rows: float32 [4, 4], P('ia'), may hold values from -0.6 to 0.6
- coupling_columns: float32 [16, 16], P(None, 'ja'), may hold values from -0.6 to 0.6
- row_neighbours: int32 [4, 16, 3], P('ia', 'ja'), may hold values from 0 to 3, as said below
- column_neighbours: int32 [4, 16, 15], P('ia', 'ja'), may hold values from 0 to 15, as said below
- row_counts: int32 [4, 16], P('ia', 'ja'), may hold values from 1 to 3
- column_counts: int32 [4, 16], P('ia', 'ja'), may hold values from 1 to 15
Outputs:
- new_amplitudes: float32 [4, 16, 128, 128], P('ia', 'ja')
- pair_energy: float32 [4, 16], P('ia', 'ja')
Inputs may be any that keep to these rules, and one draw needn't show every extreme that they name: `domain_map`: the 512 entries of one pair are distinct. `row_neighbours`: the 3 entries of a pair (i, j) are distinct and differ from i. `column_neighbours`: the 15 entries of a pair (i, j) are distinct and differ from j.
All inputs are finite; a program needn't handle non-finite values.
Results may differ from a plain program's by a relative error of at most 0.008.
Values may be sent and summed in bfloat16 or wider, within the bound.
A program may use at most 64 MiB of HBM per device.

v0:
```python
import jax
import jax.numpy as jnp
from jax import lax
from jax.sharding import PartitionSpec as P

ITERS = 2


level_shift = 0.3


def pair_intersections(packed):
    own_domain, own_basis, partner_domains, partner_bases = packed
    match = (own_domain[None, :, None] == partner_domains[:, None, :]).astype(jnp.bfloat16)
    picked = jnp.einsum(
        "suv,svb->sub", match, partner_bases, preferred_element_type=jnp.float32
    ).astype(jnp.bfloat16)
    return jnp.einsum("ua,sub->sab", own_basis, picked, preferred_element_type=jnp.float32).astype(
        jnp.bfloat16
    )


def local(
    pno_basis,
    domain_map,
    amplitudes,
    exchange_ints,
    pno_energy,
    row_energy,
    column_energy,
    coupling_rows,
    coupling_columns,
    row_neighbours,
    column_neighbours,
    row_counts,
    column_counts,
):
    pair_rows = pno_basis.shape[0]
    pair_columns = pno_basis.shape[1]
    domain_size = pno_basis.shape[2]
    width = amplitudes.shape[-1]
    total_rows = domain_map.shape[0]
    total_columns = domain_map.shape[1]
    own_pairs = pair_rows * pair_columns
    row_offset = lax.axis_index("ia") * pair_rows
    column_offset = lax.axis_index("ja") * pair_columns
    domain_rows = lax.dynamic_slice_in_dim(domain_map, row_offset, pair_rows, 0)
    domain_columns = lax.dynamic_slice_in_dim(domain_map, column_offset, pair_columns, 1)
    own_domain = lax.dynamic_slice_in_dim(domain_rows, column_offset, pair_columns, 1).reshape(
        own_pairs, domain_size
    )
    own_basis = pno_basis.reshape(own_pairs, domain_size, width)
    local_rows = jnp.arange(pair_rows, dtype=jnp.int32)[:, None, None]
    local_columns = jnp.arange(pair_columns, dtype=jnp.int32)[None, :, None]
    row_slots = (row_neighbours * pair_columns + local_columns).reshape(own_pairs, -1)
    column_slots = (local_rows * total_columns + column_neighbours).reshape(own_pairs, -1)
    row_live = (
        jnp.arange(row_neighbours.shape[2], dtype=jnp.int32)[None, None, :] < row_counts[:, :, None]
    )
    row_table = jnp.broadcast_to(coupling_rows[:, None, :], (pair_rows, pair_columns, total_rows))
    row_weight = jnp.where(row_live, jnp.take_along_axis(row_table, row_neighbours, axis=2), 0.0)
    column_live = (
        jnp.arange(column_neighbours.shape[2], dtype=jnp.int32)[None, None, :]
        < column_counts[:, :, None]
    )
    column_table = coupling_columns.T[None, :, :]
    column_weight = jnp.where(
        column_live, jnp.take_along_axis(column_table, column_neighbours, axis=2), 0.0
    )
    weights = jnp.concatenate(
        [row_weight.reshape(own_pairs, -1), column_weight.reshape(own_pairs, -1)], axis=1
    )
    partner_domains = jnp.concatenate(
        [
            domain_columns.reshape(total_rows * pair_columns, domain_size)[row_slots],
            domain_rows.reshape(pair_rows * total_columns, domain_size)[column_slots],
        ],
        axis=1,
    )

    def slot_pick(column_slab, row_slab):
        column_flat = column_slab.reshape(
            (column_slab.shape[0] * column_slab.shape[1],) + column_slab.shape[2:]
        )
        row_flat = row_slab.reshape((row_slab.shape[0] * row_slab.shape[1],) + row_slab.shape[2:])
        return jnp.concatenate([column_flat[row_slots], row_flat[column_slots]], axis=1)

    energy_gap = (
        pno_energy[:, :, :, None]
        + pno_energy[:, :, None, :]
        - row_energy[:, None, None, None]
        - column_energy[None, :, None, None]
    )
    current = amplitudes
    for iteration in range(ITERS):
        rounded = current.astype(jnp.bfloat16)
        column_bases, column_rounded = (
            lax.all_gather(pno_basis, "ia", axis=0, tiled=True),
            lax.all_gather(rounded, "ia", axis=0, tiled=True),
        )
        row_bases, row_rounded = (
            lax.all_gather(pno_basis, "ja", axis=1, tiled=True),
            lax.all_gather(rounded, "ja", axis=1, tiled=True),
        )
        partner_bases = slot_pick(column_bases, row_bases)
        intersections = lax.map(
            pair_intersections, (own_domain, own_basis, partner_domains, partner_bases)
        )
        intersection_wide = intersections.astype(jnp.float32)
        halved = jnp.einsum(
            "psab,psbc->psac",
            intersection_wide,
            slot_pick(column_rounded, row_rounded).astype(jnp.float32),
        ).astype(jnp.bfloat16)
        projected = jnp.einsum("psac,psdc->psad", halved.astype(jnp.float32), intersection_wide)
        coupled = jnp.sum(weights[:, :, None, None] * projected, axis=1).reshape(
            pair_rows, pair_columns, width, width
        )
        residual = exchange_ints + energy_gap * current - coupled
        current = current - residual / (energy_gap + level_shift)
    pair_energy = jnp.sum(
        exchange_ints * (2.0 * current - jnp.swapaxes(current, 2, 3)), axis=(2, 3)
    )
    return (current, pair_energy)


def solution(mesh):
    in_specs = (
        P("ia", "ja", None, None),
        P(),
        P("ia", "ja", None, None),
        P("ia", "ja", None, None),
        P("ia", "ja", None),
        P("ia"),
        P("ja"),
        P("ia", None),
        P(None, "ja"),
        P("ia", "ja", None),
        P("ia", "ja", None),
        P("ia", "ja"),
        P("ia", "ja"),
    )
    out_specs = (P("ia", "ja", None, None), P("ia", "ja"))
    return jax.shard_map(local, mesh=mesh, in_specs=in_specs, out_specs=out_specs, check_vma=False)
```

profile of v0, /device:TPU:0, one launch (start us, length us, event | category | flops | bytes accessed | tf_op | source)
XLA Modules:
  0.0 133.0 jit_solution(14398114743911281365)
XLA Ops:
  7.2 0.0 copy-start
  7.2 0.0 all-gather.3.cloned.1.call-start
  7.2 0.7 all-gather.3.cloned.1.call-update
  7.9 0.0 all-gather.5.cloned.1.call-start
  8.0 0.7 all-gather.5.cloned.1.call-update
  8.7 0.7 bitcast_or_fusion
  9.4 0.1 reshape.292
  9.5 0.6 gather_fusion.1
  10.2 0.1 reshape.284
  10.3 0.6 gather_fusion
  10.9 0.0 copy-done.2
  10.9 11.3 %all_gather.23 = bf16[1,16,128,128]{3,2,0,1:T(8,128)(2,1)S(1)} all-gather(bf16[1,2,128,128]{3,2,0,1:T(8,128)(2,1)S(1)} %convert_bitcast_fusion), channel_id=1, replica_groups=mesh['ia'=4,'ja'=8] {'ja'}, dimensions={1}, use_global_device_ids=true | all-gather | bytes 589824 | tf_op jit(solution)/shard_map/all_gather | solution.py:103
  22.3 0.7 gather_fusion.5
  23.0 0.0 copy-start.1
  23.0 16.9 %all_gather.22 = bf16[4,2,128,128]{3,2,1,0:T(8,128)(2,1)S(1)} all-gather(bf16[1,2,128,128]{3,2,1,0:T(8,128)(2,1)S(1)} %convert_element_type.21), channel_id=1, replica_groups=mesh['ia'=4,'ja'=8] {'ia'}, dimensions={0}, use_global_device_ids=true | all-gather | bytes 327680 | tf_op jit(solution)/shard_map/all_gather | solution.py:99
  39.9 0.6 gather_fusion.4
  40.5 0.1 reshape.348
  40.6 0.0 copy-start.11
  40.6 0.7 gather_fusion.8
  41.3 0.1 reshape.347
  41.3 0.1 reshape.356
  41.4 0.0 copy-done.1
  41.4 0.9 gather_fusion.9
  42.3 0.1 reshape.355
  43.0 0.0 copy-done.4
  43.0 0.1 copy.32
  43.2 0.1 fusion.60
  43.2 0.1 fusion.61
  43.3 0.1 pad_maximum_fusion.1
  43.4 1.1 all-gather.3.cloned.1.call-done
  44.5 1.9 %gather_fusion.2 = bf16[6,512,128]{2,1,0:T(8,128)(2,1)S(1)} fusion(bf16[8,512,128]{2,1,0:T(8,128)(2,1)} %bitcast.122, s32[1024]{0:T(1024)S(1)} %pad_clamp_fusion.1), kind=kCustom, calls=%fused_computation.2 | custom fusion | bytes 1572888 | tf_op jit(solution)/shard_map/gather | solution.py:86
  46.5 27.1 %all-gather.5.cloned.1.call-done = bf16[1,16,512,128]{3,2,0,1:T(8,128)(2,1)} async-done(((bf16[1,2,512,128]{3,2,0,1:T(8,128)(2,1)}), bf16[1,16,512,128]{3,2,0,1:T(8,128)(2,1)}) %all-gather.5.cloned.1.call-update) | async-done | bytes 2097168 | tf_op jit(solution)/shard_map/all_gather | solution.py:102
  73.6 4.6 %gather_fusion.3 = bf16[30,512,128]{2,1,0:T(8,128)(2,1)} fusion(bf16[16,512,128]{2,1,0:T(8,128)(2,1)} %bitcast.111, s32[1024]{0:T(1024)S(1)} %pad_clamp_fusion), kind=kCustom, calls=%fused_computation.3 | custom fusion | bytes 7864440 | tf_op jit(solution)/shard_map/gather | solution.py:86
  78.2 4.7 %pad_maximum_fusion = bf16[2,18,512,128]{3,2,1,0:T(8,128)(2,1)} fusion(bf16[2,15,512,128]{3,2,1,0:T(8,128)(2,1)} %bitcast.110, bf16[2,3,512,128]{3,2,1,0:T(8,128)(2,1)S(1)} %bitcast.114), kind=kLoop, calls=%fused_computation.26 | loop fusion | flops 2359296 | bytes 9437184 | tf_op jit(solution)/shard_map/concatenate | solution.py:86
  82.9 11.8 %while.2 = (s32[]{:T(128)}, bf16[2,18,128,128]{2,3,1,0:T(8,128)(2,1)}, s32[2,512]{1,0:T(2,128)S(1)}, s32[2,18,512]{2,1,0:T(8,128)S(1)}, bf16[2,18,512,128]{3,2,1...) while((s32[]{:T(128)}, bf16[2,18,128,128]{2,3,1,0:T(8,128)(2,1)}, s32[2,512]{1,0:T(2,128)S(1)}, ...), condition=%wide.region_1.2_spmd, body=%wide.region_0.0_spmd.sunk | while | flops 1516142592 | bytes 3210837 | solution.py:106
  82.9 5.9 %fusion.81 = bf16[2,18,128,128]{2,3,1,0:T(8,128)(2,1)} fusion(bf16[2,18,128,128]{2,3,1,0:T(8,128)(2,1)} %get-tuple-element.110, s32[]{:T(128)} %get-tuple-element.109, bf16[2,18,512,128]{3,2,1,0:T(8,128)(2,1)} %get-tuple-element.120, s32[18,512]{1,0:T(8,128)S(1)} %dynamic-slice_bitcast_fusion.4, s32[512]{0:T(512)S(1)} %bitcast.125, ...), kind=kOutput, calls=%fused_computation.20.clone.1 | convolution fusion | flops 1516142592 | bytes 3132928 | tf_op jit(solution)/shard_map/while/body/eval_jaxpr/ua,sub->sab/dot_general | solution.py:18
  88.9 5.8 %fusion.81 = bf16[2,18,128,128]{2,3,1,0:T(8,128)(2,1)} fusion(bf16[2,18,128,128]{2,3,1,0:T(8,128)(2,1)} %get-tuple-element.110, s32[]{:T(128)} %get-tuple-element.109, bf16[2,18,512,128]{3,2,1,0:T(8,128)(2,1)} %get-tuple-element.120, s32[18,512]{1,0:T(8,128)S(1)} %dynamic-slice_bitcast_fusion.4, s32[512]{0:T(512)S(1)} %bitcast.125, ...), kind=kOutput, calls=%fused_computation.20.clone.1 | convolution fusion | flops 1516142592 | bytes 3132928 | tf_op jit(solution)/shard_map/while/body/eval_jaxpr/ua,sub->sab/dot_general | solution.py:18
  94.7 2.6 %multiply_reduce_fusion.1 = f32[2,128,128]{2,1,0:T(8,128)S(1)} fusion(bf16[2,18,128,128]{2,3,1,0:T(8,128)(2,1)} %get-tuple-element.40, bf16[2,15,128,128]{3,2,1,0:T(8,128)(2,1)S(1)} %bitcast.117, bf16[2,3,128,128]{3,2,1,0:T(8,128)(2,1)S(1)} %bitcast.123, f32[2,18]{1,0:T(2,128)S(1)} %pad_maximum_fusion.1), kind=kOutput, calls=%fused_computation.28 | convolution fusion | flops 304316416 | bytes 2490512 | tf_op jit(solution)/shard_map/psac,psdc->psad/dot_general | solution.py:115
  97.4 0.1 fusion.66
  97.5 13.9 %all_gather.24 = bf16[4,2,128,128]{3,2,1,0:T(8,128)(2,1)S(1)} all-gather(bf16[1,2,128,128]{3,2,1,0:T(8,128)(2,1)S(1)} %get-tuple-element.59), channel_id=1, replica_groups=mesh['ia'=4,'ja'=8] {'ia'}, dimensions={0}, use_global_device_ids=true | all-gather | bytes 327680 | tf_op jit(solution)/shard_map/all_gather | solution.py:99
  111.5 9.8 %all_gather.25 = bf16[1,16,128,128]{3,2,0,1:T(8,128)(2,1)S(1)} all-gather(bf16[1,2,128,128]{3,2,0,1:T(8,128)(2,1)S(1)} %bitcast.121), channel_id=1, replica_groups=mesh['ia'=4,'ja'=8] {'ja'}, dimensions={1}, use_global_device_ids=true | all-gather | bytes 589824 | tf_op jit(solution)/shard_map/all_gather | solution.py:103
  121.3 0.7 gather_fusion.7
  122.0 0.6 gather_fusion.6
  122.6 2.6 %multiply_reduce_fusion = f32[2,128,128]{2,1,0:T(8,128)S(1)} fusion(bf16[2,18,128,128]{2,3,1,0:T(8,128)(2,1)} %get-tuple-element.40, bf16[2,15,128,128]{3,2,1,0:T(8,128)(2,1)S(1)} %bitcast.118, bf16[2,3,128,128]{3,2,1,0:T(8,128)(2,1)S(1)} %bitcast.124, f32[2,18]{1,0:T(2,128)S(1)} %pad_maximum_fusion.1), kind=kOutput, calls=%fused_computation.27 | convolution fusion | flops 304316416 | bytes 2490512 | tf_op jit(solution)/shard_map/psac,psdc->psad/dot_general | solution.py:115
  125.2 0.1 fusion.56
  125.4 0.0 copy-start.3
  125.4 0.1 copy.31
  125.5 0.6 fusion.54
  (37 shorter events, 0.2 us)
Async XLA Ops:
  7.2 2.3 %copy-start = (s32[4,16,512]{2,1,0:T(8,128)S(1)}, s32[4,16,512]{2,1,0:T(8,128)}, u32[]{:S(2)}) copy-start(s32[4,16,512]{2,1,0:T(8,128)} %param.16) | copy-start | bytes 393220
  7.2 3.0 %copy-start.7 = (s32[1,2,3]{2,1,0:T(2,128)S(1)}, s32[1,2,3]{2,1,0:T(2,128)}, u32[]{:S(2)}) copy-start(s32[1,2,3]{2,1,0:T(2,128)} %param.24) | copy-start | bytes 76
  7.2 3.7 %copy-start.2 = (f32[1,2,128,128]{3,2,1,0:T(8,128)S(1)}, f32[1,2,128,128]{3,2,1,0:T(8,128)}, u32[]{:S(2)}) copy-start(f32[1,2,128,128]{3,2,1,0:T(8,128)} %param.17) | copy-start | bytes 393220
  7.2 37.3 %all-gather.3.cloned.1.call-start = ((), (), s32[]{:S(2)}) async-start(), calls=%async_computation | async-start | bytes 1310720 | tf_op jit(solution)/shard_map/all_gather | solution.py:98
  7.9 65.7 %all-gather.5.cloned.1.call-start = ((), (), s32[]{:S(2)}) async-start(), calls=%async_computation.1 | async-start | bytes 2359296 | tf_op jit(solution)/shard_map/all_gather | solution.py:102
  22.3 18.3 %copy-start.12 = (f32[1,4]{1,0:T(1,128)S(1)}, f32[1,4]{1,0:T(1,128)}, u32[]{:S(2)}) copy-start(f32[1,4]{1,0:T(1,128)} %param.22) | copy-start | bytes 52
  23.0 18.4 %copy-start.1 = (f32[16,2]{0,1:T(2,128)S(1)}, f32[16,2]{0,1:T(2,128)}, u32[]{:S(2)}) copy-start(f32[16,2]{0,1:T(2,128)} %param.23) | copy-start | bytes 388
  39.9 3.1 %copy-start.4 = (f32[1,2,128,128]{3,2,1,0:T(8,128)S(1)}, f32[1,2,128,128]{3,2,1,0:T(8,128)}, u32[]{:S(2)}) copy-start(f32[1,2,128,128]{3,2,1,0:T(8,128)} %param.18) | copy-start | bytes 393220
  40.6 2.6 %copy-start.10 = (s32[1,2]{1,0:T(1,128)S(1)}, s32[1,2]{1,0:T(1,128)}, u32[]{:S(2)}) copy-start(s32[1,2]{1,0:T(1,128)} %param.26) | copy-start | bytes 28
  40.6 2.7 %copy-start.8 = (s32[1,2,15]{2,1,0:T(2,128)S(1)}, s32[1,2,15]{2,1,0:T(2,128)}, u32[]{:S(2)}) copy-start(s32[1,2,15]{2,1,0:T(2,128)} %param.25) | copy-start | bytes 364
  40.6 2.6 %copy-start.11 = (s32[1,2]{1,0:T(1,128)S(1)}, s32[1,2]{1,0:T(1,128)}, u32[]{:S(2)}) copy-start(s32[1,2]{1,0:T(1,128)} %param.27) | copy-start | bytes 28
  78.2 4.7 %copy-start.5 = (bf16[1,2,512,128]{3,2,1,0:T(8,128)(2,1)S(1)}, bf16[1,2,512,128]{3,2,1,0:T(8,128)(2,1)}, u32[]{:S(2)}) copy-start(bf16[1,2,512,128]{3,2,1,0:T(8,128)(2,1)} %param.15) | copy-start | bytes 786436
  94.7 2.7 %copy-start.6 = (f32[1,2,128]{2,1,0:T(2,128)S(1)}, f32[1,2,128]{2,1,0:T(2,128)}, u32[]{:S(2)}) copy-start(f32[1,2,128]{2,1,0:T(2,128)} %param.19) | copy-start | bytes 3076
  94.7 2.7 %copy-start.9 = (f32[2]{0:T(128)S(1)}, f32[2]{0:T(128)}, u32[]{:S(2)}) copy-start(f32[2]{0:T(128)} %param.21) | copy-start | bytes 28
  125.4 0.8 copy-start.3
Sparse Core Ops, SparseCore 0:
  9.6 34.9 all-gather.2
  46.4 27.1 all-gather.4
where the time goes:
time: 133 us
  blocking collectives  51.9 us (39%)
  waiting for transfers between devices  29.6 us (22%)
  matrix products  17 us (13%)
  between operations  15 us (11%)
  local copies, waits for them, and re-layouts  12.7 us (10%)
  other arithmetic  6.59 us (5%)
    all_gather x2, blocking collectives, local(): lax.all_gather(rounded, 'ia', axis=0, tiled=True)  30.8 us
    all_gather x1, waiting for transfers between devices, local(): lax.all_gather(pno_basis, 'ja', axis=1, tiled=True)  27.1 us
    all_gather x2, blocking collectives, local(): lax.all_gather(rounded, 'ja', axis=1, tiled=True)  21.1 us
    dot_general x2, matrix products, pair_intersections(): jnp.einsum('ua,sub->sab', own_basis, picked, preferred_element_type=jnp.f...  11.8 us
    gather x3, local copies, waits for them, and re-layouts, slot_pick(): row_flat[column_slots]  6.08 us
    dot_general x2, matrix products, local(): jnp.einsum('psac,psdc->psad', halved.astype(jnp.float32), intersection_wide)  5.29 us
    concatenate x1, other arithmetic, slot_pick(): jnp.concatenate([column_flat[row_slots], row_flat[column_slots]], axis=1)  4.69 us
    gather x3, local copies, waits for them, and re-layouts, slot_pick(): column_flat[row_slots]  3.09 us
  transfers between devices with their start and end apart: 2, of which 2 were waited for; matrix products, arithmetic and copies ran while one was open for 6% of the time, Pallas kernels for 0%

commit v1 on v0

v1 whole, which is shorter than its diff:
```python
import functools

import jax
import jax.numpy as jnp
from jax import lax
from jax.experimental import pallas as pl
from jax.experimental.pallas import tpu as pltpu
from jax.sharding import PartitionSpec as P

ITERS = 2
CORES = 2

level_shift = 0.3


def kernel(
    n_i,
    n_d,
    basis,
    domain,
    amplitudes,
    exchange,
    energy,
    row_energy,
    column_energy,
    coupling_rows,
    coupling_columns,
    row_nbr,
    column_nbr,
    row_cnt,
    column_cnt,
    out,
    pair_out,
    row_bases,
    col_bases,
    row_amps,
    col_amps,
    own_amps,
    basis_t,
    own_dom,
    row_pick,
    col_pick,
    inter,
    half,
    weight,
    plane_send,
    plane_recv,
    mate_send,
    mate_recv,
    up_send,
    up_recv,
    down_send,
    down_recv,
):
    z = lax.axis_index("ia")
    me = lax.axis_index("ja")
    pairs, size, width = basis.shape
    n_j = n_d * pairs
    n_c = n_d // CORES
    core = me % CORES
    chip = me // CORES
    mate = chip * CORES + (CORES - 1 - core)
    chunks = pairs + ITERS

    def chip_at(shift):
        return ((chip + shift + n_c) % n_c) * CORES + core

    def own_piece(c):
        return basis.at[c] if c < pairs else own_amps.at[c - pairs]

    def row_piece(d, c):
        return row_bases.at[d, c] if c < pairs else row_amps.at[c - pairs, d]

    def col_piece(k, c):
        return col_bases.at[k, c] if c < pairs else col_amps.at[c - pairs, k]

    def remote(src, dst, send, recv, device):
        return pltpu.make_async_remote_copy(
            src_ref=src,
            dst_ref=dst,
            send_sem=send,
            recv_sem=recv,
            device_id=device,
            device_id_type=pl.DeviceIdType.MESH,
        )

    def plane(r, c):
        return remote(
            own_piece(c),
            row_piece(me, c),
            plane_send.at[r, c],
            plane_recv.at[r, c],
            (z, chip_at(r)),
        )

    def plane_in(r, c):
        d = chip_at(-r)
        return remote(
            row_piece(d, c), row_piece(d, c), plane_send.at[r, c], plane_recv.at[r, c], (z, d)
        )

    def to_mate(r, c):
        d = chip_at(-r)
        src = own_piece(c) if r == 0 else row_piece(d, c)
        return remote(src, row_piece(d, c), mate_send.at[r, c], mate_recv.at[r, c], (z, mate))

    def mate_source(r):
        return ((chip - r + n_c) % n_c) * CORES + (CORES - 1 - core)

    def mate_in(r, c):
        d = mate_source(r)
        return remote(
            row_piece(d, c), row_piece(d, c), mate_send.at[r, c], mate_recv.at[r, c], (z, mate)
        )

    def lift(t, c, sign):
        k = z - sign * (t - 1)
        src = own_piece(c) if t == 1 else col_piece(k, c)
        send, recv = (up_send, up_recv) if sign > 0 else (down_send, down_recv)
        return remote(src, col_piece(k, c), send.at[t, c], recv.at[t, c], (z + sign, me))

    def lift_in(t, c, sign):
        k = z - sign * t
        send, recv = (up_send, up_recv) if sign > 0 else (down_send, down_recv)
        return remote(
            col_piece(k, c), col_piece(k, c), send.at[t, c], recv.at[t, c], (z - sign, me)
        )

    def has_source(t, sign):
        return z >= t if sign > 0 else z + t <= n_i - 1

    def has_target(sign):
        return z <= n_i - 2 if sign > 0 else z >= 1

    def send_own(c):
        for sign in (1, -1):

            @pl.when(has_target(sign))
            def _():
                lift(1, c, sign).start()

        for r in range(1, n_c):
            plane(r, c).start()
        to_mate(0, c).start()

    def pass_column(t, c):
        for sign in (1, -1):

            @pl.when(has_source(t, sign))
            def _():
                lift_in(t, c, sign).wait_recv()

            if t + 1 < n_i:

                @pl.when(jnp.logical_and(has_source(t, sign), has_target(sign)))
                def _():
                    lift(t + 1, c, sign).start()

    def pass_row(r, c):
        plane_in(r, c).wait_recv()
        to_mate(r, c).start()

    barrier = pltpu.get_barrier_semaphore()

    def greet(device):
        pl.semaphore_signal(
            barrier, inc=1, device_id=device, device_id_type=pl.DeviceIdType.MESH
        )

    greet((z, mate))
    for r in range(1, n_c):
        greet((z, chip_at(r)))
    for sign in (1, -1):

        @pl.when(has_target(sign))
        def _():
            greet((z + sign, me))

    ends = (z + n_i - 1) // n_i + (2 * n_i - 2 - z) // n_i
    pl.semaphore_wait(barrier, n_c + ends)

    for c in range(pairs):
        send_own(c)

    for p in range(pairs):
        own_amps[0, p] = amplitudes[p].astype(jnp.bfloat16)
        basis_t[p] = basis[p].astype(jnp.float32).T.astype(jnp.bfloat16)
        entries = domain[z, pl.ds(me * pairs + p, 1), :]
        own_dom[p] = jnp.broadcast_to(entries, (width, size)).T

    for p in range(pairs):
        slots = column_nbr.shape[1]
        names = lax.broadcasted_iota(jnp.int32, (n_j, slots), 0)
        order = lax.broadcasted_iota(jnp.int32, (n_j, slots), 1)
        hit = jnp.logical_and(column_nbr[p : p + 1, :] == names, order < column_cnt[0, p])
        chosen = jnp.sum(jnp.where(hit, 1.0, 0.0), axis=1, keepdims=True)
        weight[p, 0:n_j, :] = jnp.broadcast_to(
            chosen * coupling_columns[:, p : p + 1], (n_j, width)
        )
        slots = row_nbr.shape[1]
        names = lax.broadcasted_iota(jnp.int32, (n_i, slots), 0)
        order = lax.broadcasted_iota(jnp.int32, (n_i, slots), 1)
        hit = jnp.logical_and(row_nbr[p : p + 1, :] == names, order < row_cnt[0, p])
        chosen = jnp.sum(jnp.where(hit, 1.0, 0.0), axis=1, keepdims=True)
        diagonal = lax.broadcasted_iota(jnp.int32, (n_i, n_i), 0) == lax.broadcasted_iota(
            jnp.int32, (n_i, n_i), 1
        )
        table = jnp.sum(
            jnp.where(diagonal, coupling_rows[...], 0.0), axis=1, keepdims=True
        )
        weight[p, n_j : n_j + n_i, :] = jnp.broadcast_to(chosen * table, (n_i, width))

    def picked(p, entries):
        own = jnp.concatenate([own_dom[p]] * (size // width), axis=1)
        match = jnp.where(own == entries, 1.0, 0.0).astype(jnp.bfloat16)
        return jnp.dot(basis_t[p], match, preferred_element_type=jnp.float32).astype(
            jnp.bfloat16
        )

    def pick_row(q, carry):
        entries = domain[z, pl.ds(q, 1), :]
        for p in range(pairs):
            row_pick[q, p * width : (p + 1) * width, :] = picked(p, entries)
        return carry

    def pick_col(k, carry):
        for p in range(pairs):
            entries = domain[k, pl.ds(me * pairs + p, 1), :]
            col_pick[k, p * width : (p + 1) * width, :] = picked(p, entries)
        return carry

    def lanes(q):
        return pl.ds(pl.multiple_of(q * width, width), width)

    def intersect_row(d, c, bases):
        q = d * pairs + c
        found = jnp.dot(row_pick[q], bases, preferred_element_type=jnp.float32)
        inter[:, lanes(q)] = found.astype(jnp.bfloat16)

    def intersect_col(k, c):
        rows = slice(c * width, (c + 1) * width)
        found = jnp.dot(
            col_pick[k, rows, :], col_bases[k, c], preferred_element_type=jnp.float32
        )
        inter[rows, lanes(n_j + k)] = found.astype(jnp.bfloat16)

    third = n_j // 4
    lax.fori_loop(0, third, pick_row, 0)
    for c in range(pairs):
        send_c = c
        pass_column(1, send_c)
        for r in range(1, n_c):
            pass_row(r, send_c)
        if c == 0:
            send_own(pairs)
        lax.fori_loop((c + 1) * third, (c + 2) * third, pick_row, 0)
    lax.fori_loop((pairs + 1) * third, n_j, pick_row, 0)
    lax.fori_loop(0, n_i, pick_col, 0)

    zero = jnp.zeros((pairs * width, width), jnp.bfloat16)
    inter[:, lanes(n_j + z)] = zero
    half[:, lanes(n_j + z)] = zero
    for c in range(pairs):
        intersect_row(me, c, basis[c])
    for t in range(1, n_i):
        for c in range(pairs):
            if t > 1:
                pass_column(t, c)
            for sign in (1, -1):

                @pl.when(has_source(t, sign))
                def _():
                    intersect_col(z - sign * t, c)

        pass_column(t, pairs)
        if t == 1:
            for r in range(1, n_c):
                pass_row(r, pairs)
            for r in range(1, n_c):
                for c in range(pairs):
                    d = chip_at(-r)
                    intersect_row(d, c, row_bases[d, c])
            for r in range(n_c):
                for c in range(pairs):
                    d = mate_source(r)
                    mate_in(r, c).wait_recv()
                    intersect_row(d, c, row_bases[d, c])
                mate_in(r, pairs).wait_recv()

    def halve_row(it, d, amps):
        for c in range(pairs):
            q = d * pairs + c
            both = jnp.dot(inter[:, lanes(q)], amps[c], preferred_element_type=jnp.float32)
            for p in range(pairs):
                rows = slice(p * width, (p + 1) * width)
                half[rows, lanes(q)] = (both[rows] * weight[p, pl.ds(q, 1), :]).astype(
                    jnp.bfloat16
                )

    def halve_col(it, k):
        for p in range(pairs):
            rows = slice(p * width, (p + 1) * width)
            one = jnp.dot(
                inter[rows, lanes(n_j + k)],
                col_amps[it, k, p],
                preferred_element_type=jnp.float32,
            )
            half[rows, lanes(n_j + k)] = (one * weight[p, pl.ds(n_j + k, 1), :]).astype(
                jnp.bfloat16
            )

    for it in range(ITERS):
        c = pairs + it
        if it > 0:
            send_own(c)
        halve_row(it, me, own_amps.at[it])
        if it > 0:
            pass_column(1, c)
        for r in range(1, n_c):
            if it > 0:
                pass_row(r, c)
        for t in range(1, n_i):
            if it > 0 and t > 1:
                pass_column(t, c)
            if t == 1:
                for r in range(1, n_c):
                    d = chip_at(-r)
                    halve_row(it, d, row_amps.at[it, d])
            for sign in (1, -1):

                @pl.when(has_source(t, sign))
                def _():
                    halve_col(it, z - sign * t)

        for r in range(n_c):
            if it > 0:
                mate_in(r, c).wait_recv()
            d = mate_source(r)
            halve_row(it, d, row_amps.at[it, d])
        for p in range(pairs):
            rows = slice(p * width, (p + 1) * width)
            coupled = lax.dot_general(
                half[rows, :],
                inter[rows, :],
                (((1,), (1,)), ((), ())),
                preferred_element_type=jnp.float32,
            )
            across = jnp.broadcast_to(energy[p : p + 1, :], (width, width))
            gap = across.T + across - row_energy[0] - column_energy[p]
            current = amplitudes[p] if it == 0 else out[p]
            residual = exchange[p] + gap * current - coupled
            current = current - residual / (gap + level_shift)
            out[p] = current
            if it + 1 < ITERS:
                own_amps[it + 1, p] = current.astype(jnp.bfloat16)
            else:
                terms = exchange[p] * (2.0 * current - current.T)
                pair_out[:, p : p + 1] = jnp.sum(
                    jnp.sum(terms, axis=0, keepdims=True), axis=1, keepdims=True
                )

    for c in range(chunks):
        for r in range(1, n_c):
            plane(r, c).wait_send()
        for r in range(n_c):
            to_mate(r, c).wait_send()
        for sign in (1, -1):

            @pl.when(has_target(sign))
            def _():
                lift(1, c, sign).wait_send()

            for t in range(1, n_i - 1):

                @pl.when(jnp.logical_and(has_source(t, sign), has_target(sign)))
                def _():
                    lift(t + 1, c, sign).wait_send()


def local(
    n_i,
    n_d,
    pno_basis,
    domain_map,
    amplitudes,
    exchange_ints,
    pno_energy,
    row_energy,
    column_energy,
    coupling_rows,
    coupling_columns,
    row_neighbours,
    column_neighbours,
    row_counts,
    column_counts,
):
    _, pairs, size, width = pno_basis.shape
    n_j = n_d * pairs
    n_c = n_d // CORES
    chunks = pairs + ITERS
    vmem = pl.BlockSpec(memory_space=pltpu.VMEM)
    smem = pl.BlockSpec(memory_space=pltpu.SMEM)
    bf16 = jnp.bfloat16
    dma = pltpu.SemaphoreType.DMA
    new, pair_energy = pl.pallas_call(
        functools.partial(kernel, n_i, n_d),
        out_shape=(
            jax.ShapeDtypeStruct((pairs, width, width), jnp.float32),
            jax.ShapeDtypeStruct((1, pairs), jnp.float32),
        ),
        in_specs=[vmem] * 5 + [smem] * 2 + [vmem] * 4 + [smem] * 2,
        out_specs=(vmem, vmem),
        scratch_shapes=[
            pltpu.VMEM((n_d, pairs, size, width), bf16),
            pltpu.VMEM((n_i, pairs, size, width), bf16),
            pltpu.VMEM((ITERS, n_d, pairs, width, width), bf16),
            pltpu.VMEM((ITERS, n_i, pairs, width, width), bf16),
            pltpu.VMEM((ITERS, pairs, width, width), bf16),
            pltpu.VMEM((pairs, width, size), bf16),
            pltpu.VMEM((pairs, size, width), jnp.int32),
            pltpu.VMEM((n_j, pairs * width, size), bf16),
            pltpu.VMEM((n_i, pairs * width, size), bf16),
            pltpu.VMEM((pairs * width, (n_j + n_i) * width), bf16),
            pltpu.VMEM((pairs * width, (n_j + n_i) * width), bf16),
            pltpu.VMEM((pairs, n_j + n_i, width), jnp.float32),
            dma((n_c, chunks)),
            dma((n_c, chunks)),
            dma((n_c, chunks)),
            dma((n_c, chunks)),
            dma((n_i, chunks)),
            dma((n_i, chunks)),
            dma((n_i, chunks)),
            dma((n_i, chunks)),
        ],
        compiler_params=pltpu.CompilerParams(collective_id=0, has_side_effects=True),
        name="cepa",
    )(
        pno_basis[0],
        domain_map,
        amplitudes[0],
        exchange_ints[0],
        pno_energy[0],
        row_energy,
        column_energy,
        coupling_rows,
        coupling_columns,
        row_neighbours[0],
        column_neighbours[0],
        row_counts,
        column_counts,
    )
    return new[None], pair_energy


def solution(mesh):
    in_specs = (
        P("ia", "ja", None, None),
        P(),
        P("ia", "ja", None, None),
        P("ia", "ja", None, None),
        P("ia", "ja", None),
        P("ia"),
        P("ja"),
        P("ia", None),
        P(None, "ja"),
        P("ia", "ja", None),
        P("ia", "ja", None),
        P("ia", "ja"),
        P("ia", "ja"),
    )
    out_specs = (P("ia", "ja", None, None), P("ia", "ja"))
    body = functools.partial(local, mesh.shape["ia"], mesh.shape["ja"])
    return jax.shard_map(body, mesh=mesh, in_specs=in_specs, out_specs=out_specs, check_vma=False)
```

time: 133 us -> 56.2 us (0.42)
  blocking collectives: 51.9 us -> 0 us
  Pallas kernels: 0 us -> 51.3 us
  waiting for transfers between devices: 29.6 us -> 0 us
  matrix products: 17 us -> 0 us
  between operations: 15 us -> 1.3 us
  local copies, waits for them, and re-layouts: 12.7 us -> 3.44 us
  other arithmetic: 6.59 us -> 0 us
    all_gather x4 -> x0, blocking collectives: 51.9 us -> none  [the longest x2 30.8 us: local(): lax.all_gather(rounded, 'ia', axis=0, tiled=True)]
    pallas_call x0 -> x1, Pallas kernels: none -> 51.3 us  [local(): pl.pallas_call(functools.partial(kernel, n_i, n_d), out_shape=(jax.ShapeD...]
    all_gather x2 -> x0, waiting for transfers between devices: 28.3 us -> none  [the longest x1 27.1 us: local(): lax.all_gather(pno_basis, 'ja', axis=1, tiled=True)]
    dot_general x4 -> x0, matrix products: 17 us -> none  [the longest x2 11.8 us: pair_intersections(): jnp.einsum('ua,sub->sab', own_basis, picked, preferred_element_type=jnp.f...]
    gather x16 -> x0, local copies, waits for them, and re-layouts: 12.2 us -> none  [the longest x3 6.08 us: slot_pick(): row_flat[column_slots]]
    concatenate x3 -> x0, other arithmetic: 4.78 us -> none  [the longest x1 4.69 us: slot_pick(): jnp.concatenate([column_flat[row_slots], row_flat[column_slots]], axis=1)]
    unnamed x27 -> x7, local copies, waits for them, and re-layouts: 0.16 us -> 3.44 us
    unnamed x2 -> x0, waiting for transfers between devices: 1.38 us -> none
  transfers between devices with their start and end apart: 2 -> 0, of which waited for: 2 -> 0; matrix products, arithmetic and copies ran while one was open for 6% -> 0% of each run, Pallas kernels for 0% -> 0%
where the time goes in v1:
time: 56.2 us; the launch traced here: 56 us
  Pallas kernels  51.3 us (91%)
  local copies, waits for them, and re-layouts  3.44 us (6%)
  between operations  1.3 us (2%)
    pallas_call x1, Pallas kernels, local(): pl.pallas_call(functools.partial(kernel, n_i, n_d), out_shape=(jax.ShapeD...  51.3 us
    unnamed x7, local copies, waits for them, and re-layouts  3.44 us

profile of v1, /device:TPU:0, one launch (start us, length us, event | category | flops | bytes accessed | tf_op | source)
XLA Modules:
  0.0 56.0 jit_solution(8737661277486318560)
XLA Ops:
  1.3 0.0 copy-start
  1.3 0.7 %copy-done = f32[16,2]{0,1:T(2,128)S(1)} copy-done((f32[16,2]{0,1:T(2,128)S(1)}, f32[16,2]{0,1:T(2,128)}, u32[]{:S(2)}) %copy-start) | copy-done | bytes 152
  2.0 0.7 %copy.15.coupling_columns = f32[16,2]{1,0:T(8,128)} copy(f32[16,2]{0,1:T(2,128)S(1)} %copy-done) | data formatting | bytes 256 | tf_op args[8]
  2.6 51.3 %cepa.1 = (f32[2,128,128]{2,1,0:T(8,128)}, f32[1,2]{1,0:T(1,128)}) custom-call(bf16[2,512,128]{2,1,0:T(8,128)(2,1)} %bitcast.7, s32[4,16,512]{2,1,0:T(8,128)} %domain.1, f32[2,128,128]{2,1,0:T(8,128)} %bitcast.9, f32[2,128,128]{2,1,0:T(8,128)} %bitcast.10, f32[2,128]{1,0:T(2,128)} %bitcast.11, f32[1]{0:T(128)S(6)} %copy.18.row_energy, f32[2]{0:T(128)} %column_energy.1, ...), custom_call_target="tpu_custom_call" | custom-call | tf_op jit(solution)/shard_map/cepa/pallas_call | solution.py:405
  53.9 0.0 copy-start.1
  53.9 1.6 %copy.19 = f32[1,2,128,128]{3,2,1,0:T(8,128)} copy(f32[1,2,128,128]{3,2,1,0:T(8,128)} %bitcast.8) | data formatting | bytes 262144
  55.5 0.0 copy-done.1
  55.5 0.5 copy.20
Async XLA Ops:
  1.3 0.7 %copy-start = (f32[16,2]{0,1:T(2,128)S(1)}, f32[16,2]{0,1:T(2,128)}, u32[]{:S(2)}) copy-start(f32[16,2]{0,1:T(2,128)} %param.21) | copy-start | bytes 388
  53.9 1.6 %copy-start.1 = (f32[1,2]{1,0:T(1,128)S(1)}, f32[1,2]{1,0:T(1,128)}, u32[]{:S(2)}) copy-start(f32[1,2]{1,0:T(1,128)} %get-tuple-element.9) | copy-start | bytes 28

commit v2 on v1

--- a/solution.py
+++ b/solution.py
@@ -43,6 +43,8 @@
     inter,
     half,
     weight,
+    back_out,
+    back_in,
     plane_send,
     plane_recv,
     mate_send,
@@ -51,6 +53,8 @@
     up_recv,
     down_send,
     down_recv,
+    back_send,
+    back_recv,
 ):
     z = lax.axis_index("ia")
     me = lax.axis_index("ja")
@@ -62,8 +66,20 @@
     mate = chip * CORES + (CORES - 1 - core)
     chunks = pairs + ITERS
 
+    side = round(n_c**0.5)
+    side = side if side * side == n_c else n_c
+
+    def snake(place):
+        line, step = place // side, place % side
+        odd = line % 2
+        return line * side + step + odd * (side - 1 - 2 * step)
+
+    spot = snake(chip)
+
     def chip_at(shift):
-        return ((chip + shift + n_c) % n_c) * CORES + core
+        return snake((spot + shift + n_c) % n_c) * CORES + core
+
+    relayed = n_c == 4
 
     def own_piece(c):
         return basis.at[c] if c < pairs else own_amps.at[c - pairs]
@@ -93,6 +109,20 @@
             (z, chip_at(r)),
         )
 
+    def corner(c):
+        way = 1 if c % 2 == 0 else -1
+        d = chip_at(-way)
+        return remote(
+            row_piece(d, c),
+            row_piece(d, c),
+            plane_send.at[2, c],
+            plane_recv.at[2, c],
+            (z, chip_at(way)),
+        )
+
+    def is_corner(r, c):
+        return relayed and r == 2 and c < pairs
+
     def plane_in(r, c):
         d = chip_at(-r)
         return remote(
@@ -105,7 +135,7 @@
         return remote(src, row_piece(d, c), mate_send.at[r, c], mate_recv.at[r, c], (z, mate))
 
     def mate_source(r):
-        return ((chip - r + n_c) % n_c) * CORES + (CORES - 1 - core)
+        return snake((spot - r + n_c) % n_c) * CORES + (CORES - 1 - core)
 
     def mate_in(r, c):
         d = mate_source(r)
@@ -126,39 +156,87 @@
             col_piece(k, c), col_piece(k, c), send.at[t, c], recv.at[t, c], (z - sign, me)
         )
 
-    def has_source(t, sign):
-        return z >= t if sign > 0 else z + t <= n_i - 1
-
-    def has_target(sign):
-        return z <= n_i - 2 if sign > 0 else z >= 1
+    def place(sign):
+        return z if sign > 0 else n_i - 1 - z
+
+    def is_main(c, sign):
+        return (c % 2 == 0) == (sign > 0)
+
+    def both(a, b):
+        return jnp.logical_and(a, b)
+
+    def moves(t, c, sign):
+        at = place(sign)
+        if c >= pairs or (t > 1 and is_main(c, sign)):
+            return both(at >= t - 1, at <= n_i - 2)
+        if t > 1:
+            return None
+        return at <= n_i - 3 if is_main(c, sign) else at == 0
+
+    def comes(t, c, sign):
+        at = place(sign)
+        if c >= pairs or (t > 1 and is_main(c, sign)):
+            return at >= t
+        if t > 1:
+            return None
+        return both(at >= 1, at <= n_i - 2) if is_main(c, sign) else at == 1
+
+    def returns(t, c, sign):
+        at = place(sign)
+        if t == 1:
+            return at <= n_i - 3 if is_main(c, sign) else at == 0
+        return at <= n_i - 1 - t if is_main(c, sign) else None
+
+    def when(condition, action):
+        if condition is not None:
+            pl.when(condition)(action)
+
+    def give_back(t, c, sign):
+        k = z - sign * t
+        spot_of = t + (0 if sign > 0 else n_i)
+        return remote(
+            back_out.at[k, c],
+            back_in.at[z, c],
+            back_send.at[spot_of, c],
+            back_recv.at[spot_of, c],
+            (k, me),
+        )
+
+    def take_back(t, c, sign):
+        k = z + sign * t
+        spot_of = t + (0 if sign > 0 else n_i)
+        return remote(
+            back_out.at[k, c],
+            back_in.at[k, c],
+            back_send.at[spot_of, c],
+            back_recv.at[spot_of, c],
+            (k, me),
+        )
 
     def send_own(c):
         for sign in (1, -1):
-
-            @pl.when(has_target(sign))
-            def _():
-                lift(1, c, sign).start()
-
+            when(moves(1, c, sign), lambda: lift(1, c, sign).start())
         for r in range(1, n_c):
-            plane(r, c).start()
+            if not is_corner(r, c):
+                plane(r, c).start()
         to_mate(0, c).start()
 
     def pass_column(t, c):
         for sign in (1, -1):
-
-            @pl.when(has_source(t, sign))
-            def _():
-                lift_in(t, c, sign).wait_recv()
-
-            if t + 1 < n_i:
-
-                @pl.when(jnp.logical_and(has_source(t, sign), has_target(sign)))
-                def _():
-                    lift(t + 1, c, sign).start()
+            arrives = comes(t, c, sign)
+            when(arrives, lambda: lift_in(t, c, sign).wait_recv())
+            onward = moves(t + 1, c, sign) if t + 1 < n_i else None
+            if arrives is not None and onward is not None:
+                when(both(arrives, onward), lambda: lift(t + 1, c, sign).start())
 
     def pass_row(r, c):
         plane_in(r, c).wait_recv()
+        if relayed and c < pairs and r == (1 if c % 2 == 0 else n_c - 1):
+            corner(c).start()
         to_mate(r, c).start()
+
+    near = [r for r in range(1, n_c) if not is_corner(r, 0)]
+    near = near + [r for r in range(1, n_c) if is_corner(r, 0)]
 
     barrier = pltpu.get_barrier_semaphore()
 
@@ -170,14 +248,9 @@
     greet((z, mate))
     for r in range(1, n_c):
         greet((z, chip_at(r)))
-    for sign in (1, -1):
-
-        @pl.when(has_target(sign))
-        def _():
-            greet((z + sign, me))
-
-    ends = (z + n_i - 1) // n_i + (2 * n_i - 2 - z) // n_i
-    pl.semaphore_wait(barrier, n_c + ends)
+    for shift in range(1, n_i):
+        greet(((z + shift) % n_i, me))
+    pl.semaphore_wait(barrier, n_c + n_i - 1)
 
     for c in range(pairs):
         send_own(c)
@@ -243,57 +316,84 @@
             col_pick[k, rows, :], col_bases[k, c], preferred_element_type=jnp.float32
         )
         inter[rows, lanes(n_j + k)] = found.astype(jnp.bfloat16)
-
-    third = n_j // 4
-    lax.fori_loop(0, third, pick_row, 0)
+        back_out[k, c] = found.astype(jnp.bfloat16)
+
+    def meet_column(t, c):
+        for sign in (1, -1):
+            when(comes(t, c, sign), lambda: intersect_col(z - sign * t, c))
+
+    def return_column(t, c):
+        for sign in (1, -1):
+            when(comes(t, c, sign), lambda: give_back(t, c, sign).start())
+
+    def accept_column(t, c):
+        rows = slice(c * width, (c + 1) * width)
+        for sign in (1, -1):
+
+            def accept():
+                take_back(t, c, sign).wait_recv()
+                k = z + sign * t
+                turned = back_in[k, c].astype(jnp.float32).T
+                inter[rows, lanes(n_j + k)] = turned.astype(jnp.bfloat16)
+
+            when(returns(t, c, sign), accept)
+
+    share = n_j // 4
+    lax.fori_loop(0, n_i, pick_col, 0)
+    send_own(pairs)
     for c in range(pairs):
-        send_c = c
-        pass_column(1, send_c)
-        for r in range(1, n_c):
-            pass_row(r, send_c)
-        if c == 0:
-            send_own(pairs)
-        lax.fori_loop((c + 1) * third, (c + 2) * third, pick_row, 0)
-    lax.fori_loop((pairs + 1) * third, n_j, pick_row, 0)
-    lax.fori_loop(0, n_i, pick_col, 0)
-
+        pass_column(1, c)
+        for r in near:
+            if not is_corner(r, c):
+                pass_row(r, c)
+        meet_column(1, c)
+        lax.fori_loop(c * share, (c + 1) * share, pick_row, 0)
+        return_column(1, c)
+    pass_column(1, pairs)
     zero = jnp.zeros((pairs * width, width), jnp.bfloat16)
     inter[:, lanes(n_j + z)] = zero
     half[:, lanes(n_j + z)] = zero
     for c in range(pairs):
-        intersect_row(me, c, basis[c])
+        for r in near:
+            if is_corner(r, c):
+                pass_row(r, c)
+    for t in range(2, n_i):
+        for c in range(pairs):
+            pass_column(t, c)
+            meet_column(t, c)
+        if t == 2:
+            for r in range(1, n_c):
+                pass_row(r, pairs)
+            lax.fori_loop(pairs * share, n_j, pick_row, 0)
+            for c in range(pairs):
+                return_column(t, c)
+            for c in range(pairs):
+                intersect_row(me, c, basis[c])
+        else:
+            for c in range(pairs):
+                return_column(t, c)
+        pass_column(t, pairs)
+    for r in near:
+        for c in range(pairs):
+            d = chip_at(-r)
+            intersect_row(d, c, row_bases[d, c])
+    for r in range(n_c):
+        for c in range(pairs):
+            d = mate_source(r)
+            mate_in(r, c).wait_recv()
+            intersect_row(d, c, row_bases[d, c])
+        mate_in(r, pairs).wait_recv()
     for t in range(1, n_i):
         for c in range(pairs):
-            if t > 1:
-                pass_column(t, c)
-            for sign in (1, -1):
-
-                @pl.when(has_source(t, sign))
-                def _():
-                    intersect_col(z - sign * t, c)
-
-        pass_column(t, pairs)
-        if t == 1:
-            for r in range(1, n_c):
-                pass_row(r, pairs)
-            for r in range(1, n_c):
-                for c in range(pairs):
-                    d = chip_at(-r)
-                    intersect_row(d, c, row_bases[d, c])
-            for r in range(n_c):
-                for c in range(pairs):
-                    d = mate_source(r)
-                    mate_in(r, c).wait_recv()
-                    intersect_row(d, c, row_bases[d, c])
-                mate_in(r, pairs).wait_recv()
+            accept_column(t, c)
 
     def halve_row(it, d, amps):
         for c in range(pairs):
             q = d * pairs + c
-            both = jnp.dot(inter[:, lanes(q)], amps[c], preferred_element_type=jnp.float32)
+            pair = jnp.dot(inter[:, lanes(q)], amps[c], preferred_element_type=jnp.float32)
             for p in range(pairs):
                 rows = slice(p * width, (p + 1) * width)
-                half[rows, lanes(q)] = (both[rows] * weight[p, pl.ds(q, 1), :]).astype(
+                half[rows, lanes(q)] = (pair[rows] * weight[p, pl.ds(q, 1), :]).astype(
                     jnp.bfloat16
                 )
 
@@ -328,9 +428,7 @@
                     halve_row(it, d, row_amps.at[it, d])
             for sign in (1, -1):
 
-                @pl.when(has_source(t, sign))
-                def _():
-                    halve_col(it, z - sign * t)
+                when(comes(t, c, sign), lambda: halve_col(it, z - sign * t))
 
         for r in range(n_c):
             if it > 0:
@@ -361,20 +459,14 @@
 
     for c in range(chunks):
         for r in range(1, n_c):
-            plane(r, c).wait_send()
+            (corner(c) if is_corner(r, c) else plane(r, c)).wait_send()
         for r in range(n_c):
             to_mate(r, c).wait_send()
         for sign in (1, -1):
-
-            @pl.when(has_target(sign))
-            def _():
-                lift(1, c, sign).wait_send()
-
-            for t in range(1, n_i - 1):
-
-                @pl.when(jnp.logical_and(has_source(t, sign), has_target(sign)))
-                def _():
-                    lift(t + 1, c, sign).wait_send()
+            for t in range(1, n_i):
+                when(moves(t, c, sign), lambda: lift(t, c, sign).wait_send())
+                if c < pairs:
+                    when(comes(t, c, sign), lambda: give_back(t, c, sign).wait_send())
 
 
 def local(
@@ -423,6 +515,8 @@
             pltpu.VMEM((pairs * width, (n_j + n_i) * width), bf16),
             pltpu.VMEM((pairs * width, (n_j + n_i) * width), bf16),
             pltpu.VMEM((pairs, n_j + n_i, width), jnp.float32),
+            pltpu.VMEM((n_i, pairs, width, width), bf16),
+            pltpu.VMEM((n_i, pairs, width, width), bf16),
             dma((n_c, chunks)),
             dma((n_c, chunks)),
             dma((n_c, chunks)),
@@ -431,6 +525,8 @@
             dma((n_i, chunks)),
             dma((n_i, chunks)),
             dma((n_i, chunks)),
+            dma((2 * n_i, pairs)),
+            dma((2 * n_i, pairs)),
         ],
         compiler_params=pltpu.CompilerParams(collective_id=0, has_side_effects=True),
         name="cepa",

time: 56.2 us -> 49.1 us (0.87)
  Pallas kernels: 51.3 us -> 44.2 us
    pallas_call x1, Pallas kernels: 51.3 us -> 44.2 us  [local(): pl.pallas_call(functools.partial(kernel, n_i, n_d), out_shape=(jax.ShapeD...]
where the time goes in v2:
time: 49.1 us; the launch traced here: 48.9 us
  Pallas kernels  44.2 us (90%)
  local copies, waits for them, and re-layouts  3.44 us (7%)
  between operations  1.3 us (3%)
    pallas_call x1, Pallas kernels, local(): pl.pallas_call(functools.partial(kernel, n_i, n_d), out_shape=(jax.ShapeD...  44.2 us
    unnamed x7, local copies, waits for them, and re-layouts  3.44 us

profile of v2, /device:TPU:0, one launch (start us, length us, event | category | flops | bytes accessed | tf_op | source)
XLA Modules:
  0.0 48.9 jit_solution(3458739438178727254)
XLA Ops:
  1.3 0.0 copy-start
  1.3 0.7 %copy-done = f32[16,2]{0,1:T(2,128)S(1)} copy-done((f32[16,2]{0,1:T(2,128)S(1)}, f32[16,2]{0,1:T(2,128)}, u32[]{:S(2)}) %copy-start) | copy-done | bytes 152
  2.0 0.7 %copy.15.coupling_columns = f32[16,2]{1,0:T(8,128)} copy(f32[16,2]{0,1:T(2,128)S(1)} %copy-done) | data formatting | bytes 256 | tf_op args[8]
  2.6 44.2 %cepa.1 = (f32[2,128,128]{2,1,0:T(8,128)}, f32[1,2]{1,0:T(1,128)}) custom-call(bf16[2,512,128]{2,1,0:T(8,128)(2,1)} %bitcast.7, s32[4,16,512]{2,1,0:T(8,128)} %domain.1, f32[2,128,128]{2,1,0:T(8,128)} %bitcast.9, f32[2,128,128]{2,1,0:T(8,128)} %bitcast.10, f32[2,128]{1,0:T(2,128)} %bitcast.11, f32[1]{0:T(128)S(6)} %copy.18.row_energy, f32[2]{0:T(128)} %column_energy.1, ...), custom_call_target="tpu_custom_call" | custom-call | tf_op jit(solution)/shard_map/cepa/pallas_call | solution.py:497
  46.8 0.0 copy-start.1
  46.8 1.6 %copy.19 = f32[1,2,128,128]{3,2,1,0:T(8,128)} copy(f32[1,2,128,128]{3,2,1,0:T(8,128)} %bitcast.8) | data formatting | bytes 262144
  48.4 0.0 copy-done.1
  48.4 0.5 %copy.20 = f32[1,2]{1,0:T(1,128)} copy(f32[1,2]{1,0:T(1,128)S(1)} %copy-done.1) | data formatting | bytes 16
Async XLA Ops:
  1.3 0.7 %copy-start = (f32[16,2]{0,1:T(2,128)S(1)}, f32[16,2]{0,1:T(2,128)}, u32[]{:S(2)}) copy-start(f32[16,2]{0,1:T(2,128)} %param.21) | copy-start | bytes 388
  46.8 1.6 %copy-start.1 = (f32[1,2]{1,0:T(1,128)S(1)}, f32[1,2]{1,0:T(1,128)}, u32[]{:S(2)}) copy-start(f32[1,2]{1,0:T(1,128)} %get-tuple-element.9) | copy-start | bytes 28

commit v3 on v2

--- a/solution.py
+++ b/solution.py
@@ -9,6 +9,7 @@
 
 ITERS = 2
 CORES = 2
+SPLIT = 1
 
 level_shift = 0.3
 
@@ -143,18 +144,36 @@
             row_piece(d, c), row_piece(d, c), mate_send.at[r, c], mate_recv.at[r, c], (z, mate)
         )
 
-    def lift(t, c, sign):
-        k = z - sign * (t - 1)
-        src = own_piece(c) if t == 1 else col_piece(k, c)
+    def direct(c):
+        return c >= pairs
+
+    def parts(c):
+        return range(SPLIT if c < pairs else 1)
+
+    def part(ref, c, h):
+        rows = size // SPLIT
+        return ref.at[pl.ds(h * rows, rows)] if c < pairs else ref
+
+    def lift(t, c, sign, h):
+        alone = direct(c) or t == 1
+        k = z if alone else z - sign * (t - 1)
+        src = own_piece(c) if alone else col_piece(k, c)
         send, recv = (up_send, up_recv) if sign > 0 else (down_send, down_recv)
-        return remote(src, col_piece(k, c), send.at[t, c], recv.at[t, c], (z + sign, me))
-
-    def lift_in(t, c, sign):
+        slot = c * SPLIT + h
+        return remote(
+            part(src, c, h),
+            part(col_piece(k, c), c, h),
+            send.at[t, slot],
+            recv.at[t, slot],
+            (z + sign * (t if direct(c) else 1), me),
+        )
+
+    def lift_in(t, c, sign, h):
         k = z - sign * t
         send, recv = (up_send, up_recv) if sign > 0 else (down_send, down_recv)
-        return remote(
-            col_piece(k, c), col_piece(k, c), send.at[t, c], recv.at[t, c], (z - sign, me)
-        )
+        slot = c * SPLIT + h
+        block = part(col_piece(k, c), c, h)
+        return remote(block, block, send.at[t, slot], recv.at[t, slot], (z - sign, me))
 
     def place(sign):
         return z if sign > 0 else n_i - 1 - z
@@ -167,6 +186,8 @@
 
     def moves(t, c, sign):
         at = place(sign)
+        if direct(c):
+            return at <= n_i - 1 - t
         if c >= pairs or (t > 1 and is_main(c, sign)):
             return both(at >= t - 1, at <= n_i - 2)
         if t > 1:
@@ -214,20 +235,23 @@
         )
 
     def send_own(c):
-        for sign in (1, -1):
-            when(moves(1, c, sign), lambda: lift(1, c, sign).start())
+        for t in reversed(range(1, n_i if direct(c) else 2)):
+            for sign in (1, -1):
+                for h in parts(c):
+                    when(moves(t, c, sign), lambda: lift(t, c, sign, h).start())
         for r in range(1, n_c):
             if not is_corner(r, c):
                 plane(r, c).start()
         to_mate(0, c).start()
 
     def pass_column(t, c):
-        for sign in (1, -1):
-            arrives = comes(t, c, sign)
-            when(arrives, lambda: lift_in(t, c, sign).wait_recv())
-            onward = moves(t + 1, c, sign) if t + 1 < n_i else None
-            if arrives is not None and onward is not None:
-                when(both(arrives, onward), lambda: lift(t + 1, c, sign).start())
+        for h in parts(c):
+            for sign in (1, -1):
+                arrives = comes(t, c, sign)
+                when(arrives, lambda: lift_in(t, c, sign, h).wait_recv())
+                onward = moves(t + 1, c, sign) if t + 1 < n_i and not direct(c) else None
+                if arrives is not None and onward is not None:
+                    when(both(arrives, onward), lambda: lift(t + 1, c, sign, h).start())
 
     def pass_row(r, c):
         plane_in(r, c).wait_recv()
@@ -267,9 +291,13 @@
         order = lax.broadcasted_iota(jnp.int32, (n_j, slots), 1)
         hit = jnp.logical_and(column_nbr[p : p + 1, :] == names, order < column_cnt[0, p])
         chosen = jnp.sum(jnp.where(hit, 1.0, 0.0), axis=1, keepdims=True)
-        weight[p, 0:n_j, :] = jnp.broadcast_to(
-            chosen * coupling_columns[:, p : p + 1], (n_j, width)
-        )
+        diagonal = lax.broadcasted_iota(jnp.int32, (n_j, n_j), 0) == lax.broadcasted_iota(
+            jnp.int32, (n_j, n_j), 1
+        )
+        table = jnp.sum(
+            jnp.where(diagonal, coupling_columns[p : p + 1, :], 0.0), axis=1, keepdims=True
+        )
+        weight[p, 0:n_j, :] = jnp.broadcast_to(chosen * table, (n_j, width))
         slots = row_nbr.shape[1]
         names = lax.broadcasted_iota(jnp.int32, (n_i, slots), 0)
         order = lax.broadcasted_iota(jnp.int32, (n_i, slots), 1)
@@ -415,26 +443,21 @@
             send_own(c)
         halve_row(it, me, own_amps.at[it])
         if it > 0:
-            pass_column(1, c)
+            for r in range(1, n_c):
+                pass_row(r, c)
         for r in range(1, n_c):
-            if it > 0:
-                pass_row(r, c)
-        for t in range(1, n_i):
-            if it > 0 and t > 1:
-                pass_column(t, c)
-            if t == 1:
-                for r in range(1, n_c):
-                    d = chip_at(-r)
-                    halve_row(it, d, row_amps.at[it, d])
-            for sign in (1, -1):
-
-                when(comes(t, c, sign), lambda: halve_col(it, z - sign * t))
-
+            d = chip_at(-r)
+            halve_row(it, d, row_amps.at[it, d])
         for r in range(n_c):
             if it > 0:
                 mate_in(r, c).wait_recv()
             d = mate_source(r)
             halve_row(it, d, row_amps.at[it, d])
+        for t in range(1, n_i):
+            if it > 0:
+                pass_column(t, c)
+            for sign in (1, -1):
+                when(comes(t, c, sign), lambda: halve_col(it, z - sign * t))
         for p in range(pairs):
             rows = slice(p * width, (p + 1) * width)
             coupled = lax.dot_general(
@@ -464,7 +487,8 @@
             to_mate(r, c).wait_send()
         for sign in (1, -1):
             for t in range(1, n_i):
-                when(moves(t, c, sign), lambda: lift(t, c, sign).wait_send())
+                for h in parts(c):
+                    when(moves(t, c, sign), lambda: lift(t, c, sign, h).wait_send())
                 if c < pairs:
                     when(comes(t, c, sign), lambda: give_back(t, c, sign).wait_send())
 
@@ -521,10 +545,10 @@
             dma((n_c, chunks)),
             dma((n_c, chunks)),
             dma((n_c, chunks)),
-            dma((n_i, chunks)),
-            dma((n_i, chunks)),
-            dma((n_i, chunks)),
-            dma((n_i, chunks)),
+            dma((n_i, chunks * SPLIT)),
+            dma((n_i, chunks * SPLIT)),
+            dma((n_i, chunks * SPLIT)),
+            dma((n_i, chunks * SPLIT)),
             dma((2 * n_i, pairs)),
             dma((2 * n_i, pairs)),
         ],
@@ -539,7 +563,7 @@
         row_energy,
         column_energy,
         coupling_rows,
-        coupling_columns,
+        coupling_columns.T,
         row_neighbours[0],
         column_neighbours[0],
         row_counts,

time: 49.1 us -> 41.7 us (0.85)
  Pallas kernels: 44.2 us -> 38 us
  local copies, waits for them, and re-layouts: 3.44 us -> 2.08 us
    pallas_call x1, Pallas kernels: 44.2 us -> 38 us  [local(): pl.pallas_call(functools.partial(kernel, n_i, n_d), out_shape=(jax.ShapeD...]
    unnamed x7 -> x4, local copies, waits for them, and re-layouts: 3.44 us -> 2.08 us
where the time goes in v3:
time: 41.7 us; the launch traced here: 41.4 us
  Pallas kernels  38 us (91%)
  local copies, waits for them, and re-layouts  2.08 us (5%)
  between operations  1.3 us (3%)
    pallas_call x1, Pallas kernels, local(): pl.pallas_call(functools.partial(kernel, n_i, n_d), out_shape=(jax.ShapeD...  38 us
    unnamed x4, local copies, waits for them, and re-layouts  2.08 us

profile of v3, /device:TPU:0, one launch (start us, length us, event | category | flops | bytes accessed | tf_op | source)
XLA Modules:
  0.0 41.4 jit_solution(15122866288526687063)
XLA Ops:
  1.3 38.0 %cepa.1 = (f32[2,128,128]{2,1,0:T(8,128)}, f32[1,2]{1,0:T(1,128)}) custom-call(bf16[2,512,128]{2,1,0:T(8,128)(2,1)} %bitcast.8, s32[4,16,512]{2,1,0:T(8,128)} %domain.1, f32[2,128,128]{2,1,0:T(8,128)} %bitcast.10, f32[2,128,128]{2,1,0:T(8,128)} %bitcast.11, f32[2,128]{1,0:T(2,128)} %bitcast.12, f32[1]{0:T(128)S(6)} %copy.17.row_energy, f32[2]{0:T(128)} %column_energy.1, ...), custom_call_target="tpu_custom_call" | custom-call | tf_op jit(solution)/shard_map/cepa/pallas_call | solution.py:521
  39.3 0.0 copy-start
  39.3 1.6 %copy.18 = f32[1,2,128,128]{3,2,1,0:T(8,128)} copy(f32[1,2,128,128]{3,2,1,0:T(8,128)} %bitcast.9) | data formatting | bytes 262144
  40.9 0.0 copy-done
  40.9 0.5 %copy.19 = f32[1,2]{1,0:T(1,128)} copy(f32[1,2]{1,0:T(1,128)S(1)} %copy-done) | data formatting | bytes 16
Async XLA Ops:
  39.3 1.6 %copy-start = (f32[1,2]{1,0:T(1,128)S(1)}, f32[1,2]{1,0:T(1,128)}, u32[]{:S(2)}) copy-start(f32[1,2]{1,0:T(1,128)} %get-tuple-element.9) | copy-start | bytes 28
